TPU v7x, 256 devices: a whole 4x4x8 slice. The times are simulated.
256 devices in a mesh: req: 64 (over x_lo, y, z), ctx: 4 (over x_hi, core).
Axes of the slice: x: 4 (x_hi: 2, x_lo: 2; x = x_hi * 2 + x_lo), y: 4, z: 8, core: 2. Of those that a mesh axis runs over, the one named last changes fastest.
Arguments:
- q_nope: bfloat16 [64, 128, 8192], P('req'), may hold values from -6 to 6
- q_rope: bfloat16 [64, 128, 4096], P('req'), may hold values from -600 to 600
- cache_latent: bfloat16 [64, 1024, 512], P('req', 'ctx'), may hold values from -6 to 6
- cache_rope: bfloat16 [64, 1024, 64], P('req', 'ctx'), may hold values from -4 to 4
- new_latent: bfloat16 [64, 128, 512], P('req', 'ctx'), may hold values from -6 to 6
- new_rope: bfloat16 [64, 128, 64], P('req', 'ctx'), may hold values from -8 to 8
- lengths: int32 [64, 4], P('req', 'ctx'), may hold values from 64 to 256, as said below
- w_key: bfloat16 [512, 8192], P(None, 'ctx'), may hold values from -0.25 to 0.25
- w_value: bfloat16 [512, 8192], P(None, 'ctx'), may hold values from -0.25 to 0.25
Outputs:
- attended: bfloat16 [64, 128, 8192], P('req', None, 'ctx')
Inputs may be any that keep to these rules, and one draw needn't show every extreme that they name: lengths[r, g] counts the live cached rows at the start of request r's slots in context group g; all cached rows precede the new tokens; some entry equals 256 in every draw.
All inputs are finite; a program needn't handle non-finite values.
Results may differ from a plain program's by a relative error of at most 0.015.
Values may be sent and summed in bfloat16 or wider, within the bound.
A program may use at most 128 MiB of HBM per device.

v0:
```python
import math
import jax
import jax.numpy as jnp
from jax import lax
from jax.sharding import PartitionSpec as P

DR = 64
DH = 128
DV = 128
HEADS = 64
GROUP = 4
BLOCK = 256
blocked_score = -1e30


def expand_block(
    lat_rows, rope_keys, visible, query_nope, query_rope, weight_key, weight_value, running
):
    running_max, running_sum, running_out = running
    row_count = lat_rows.shape[0]
    score_scale = 1.0 / math.sqrt(DH + DR)
    key_rows = jnp.dot(lat_rows, weight_key, preferred_element_type=jnp.float32).astype(
        jnp.bfloat16
    )
    value_rows = jnp.dot(lat_rows, weight_value, preferred_element_type=jnp.float32).astype(
        jnp.bfloat16
    )
    key_rows = key_rows.reshape(row_count, GROUP, DH)
    value_rows = value_rows.reshape(row_count, GROUP, DV)
    scores = jnp.einsum("qhd,khd->qhk", query_nope, key_rows, preferred_element_type=jnp.float32)
    scores = scores + jnp.einsum(
        "qhd,kd->qhk", query_rope, rope_keys, preferred_element_type=jnp.float32
    )
    scores = jnp.where(visible[:, None, :], scores * score_scale, blocked_score)
    new_max = jnp.maximum(running_max, jnp.max(scores, axis=-1))
    factor = jnp.exp(running_max - new_max)
    weights = jnp.where(visible[:, None, :], jnp.exp(scores - new_max[..., None]), 0.0)
    running_sum = running_sum * factor + jnp.sum(weights, axis=-1)
    running_out = running_out * factor[..., None] + jnp.einsum(
        "qhk,khd->qhd", weights.astype(jnp.bfloat16), value_rows, preferred_element_type=jnp.float32
    )
    return (new_max, running_sum, running_out)


def start_running(query_count):
    return (
        jnp.full((query_count, GROUP), blocked_score, jnp.float32),
        jnp.zeros((query_count, GROUP), jnp.float32),
        jnp.zeros((query_count, GROUP, DV), jnp.float32),
    )


def cached_pass(
    running, query_nope, query_rope, weight_key, weight_value, cache_rows, cache_keys, live_rows
):

    def advance(block_index, running):
        offset = block_index * BLOCK
        visible = (offset + jnp.arange(BLOCK, dtype=jnp.int32))[None, :] < live_rows
        visible = jnp.broadcast_to(visible, (query_nope.shape[0], BLOCK))
        return expand_block(
            cache_rows,
            cache_keys,
            visible,
            query_nope,
            query_rope,
            weight_key,
            weight_value,
            running,
        )

    block_count = (live_rows + BLOCK - 1) // BLOCK
    return lax.fori_loop(0, block_count, advance, running)


def fresh_pass(
    running, query_nope, query_rope, weight_key, weight_value, fresh_rows, fresh_keys, fresh_first
):
    query_count = query_nope.shape[0]
    fresh_index = fresh_first + jnp.arange(fresh_rows.shape[0], dtype=jnp.int32)
    visible = fresh_index[None, :] <= jnp.arange(query_count, dtype=jnp.int32)[:, None]
    return expand_block(
        fresh_rows, fresh_keys, visible, query_nope, query_rope, weight_key, weight_value, running
    )


def shards(q_nope, q_rope, cache_latent, cache_rope, new_latent, new_rope, lengths, w_key, w_value):
    ctx_count = lax.axis_size("ctx")
    ctx_index = lax.axis_index("ctx")
    queries = q_nope[0]
    rotary = q_rope[0]
    query_count = queries.shape[0]
    width_key = GROUP * DH
    width_value = GROUP * DV
    heads_here = HEADS // ctx_count
    groups = HEADS // GROUP
    fresh_rows = new_latent[0]
    fresh_first = ctx_index * fresh_rows.shape[0]
    live_rows = lengths[0, 0]
    full_key, full_value = (
        lax.all_gather(w_key, "ctx", axis=1, tiled=True),
        lax.all_gather(w_value, "ctx", axis=1, tiled=True),
    )
    maxima = []
    sums = []
    outputs = []
    for group_index in range(groups):
        weight_key = full_key[:, group_index * width_key : (group_index + 1) * width_key]
        weight_value = full_value[:, group_index * width_value : (group_index + 1) * width_value]
        query_nope = queries[:, group_index * GROUP * DH : (group_index + 1) * GROUP * DH].reshape(
            query_count, GROUP, DH
        )
        query_rope = rotary[:, group_index * GROUP * DR : (group_index + 1) * GROUP * DR].reshape(
            query_count, GROUP, DR
        )
        running = start_running(query_count)
        running = cached_pass(
            running,
            query_nope,
            query_rope,
            weight_key,
            weight_value,
            cache_latent[0],
            cache_rope[0],
            live_rows,
        )
        group_max, group_sum, group_out = fresh_pass(
            running,
            query_nope,
            query_rope,
            weight_key,
            weight_value,
            fresh_rows,
            new_rope[0],
            fresh_first,
        )
        maxima.append(group_max)
        sums.append(group_sum)
        outputs.append(group_out)
    running_max = jnp.concatenate(maxima, axis=1)
    running_sum = jnp.concatenate(sums, axis=1)
    running_out = jnp.concatenate(outputs, axis=1)
    overall_max = lax.pmax(running_max.astype(jnp.bfloat16), "ctx").astype(running_max.dtype)
    factor = jnp.exp(running_max - overall_max)
    numerator, denominator = (
        lax.psum_scatter(
            (running_out * factor[..., None]).reshape(query_count, HEADS * DV).astype(jnp.bfloat16),
            "ctx",
            scatter_dimension=1,
            tiled=True,
        ).astype(jnp.float32),
        lax.psum_scatter(
            (running_sum * factor).astype(jnp.bfloat16), "ctx", scatter_dimension=1, tiled=True
        ).astype(jnp.float32),
    )
    numerator = numerator.reshape(query_count, heads_here, DV)
    attended = (numerator / denominator[..., None]).reshape(query_count, heads_here * DV)
    return attended.astype(jnp.bfloat16)[None]


def solution(mesh):
    return jax.shard_map(
        shards,
        mesh=mesh,
        in_specs=(
            P("req", None, None),
            P("req", None, None),
            P("req", "ctx", None),
            P("req", "ctx", None),
            P("req", "ctx", None),
            P("req", "ctx", None),
            P("req", "ctx"),
            P(None, "ctx"),
            P(None, "ctx"),
        ),
        out_specs=P("req", None, "ctx"),
        check_vma=False,
    )
```

profile of v0, /device:TPU:1, one launch (start us, length us, event | category | flops | bytes accessed | tf_op | source)
XLA Modules:
  0.0 420.9 jit_solution(1115684594973445940)
XLA Ops:
  8.7 1.3 fusion.675
  18.6 3.2 copy.204
  34.6 43.7 %all-gather.3.cloned.1.call-done = bf16[512,8192]{1,0:T(8,128)(2,1)} async-done(((bf16[512,2048]{1,0:T(8,128)(2,1)}), bf16[512,8192]{1,0:T(8,128)(2,1)}) %all-gather.3.cloned.1.call-update) | async-done | bytes 8388624 | tf_op jit(solution)/shard_map/all_gather | solution.py:101
  79.5 1.7 convolution_bitcast_fusion.48
  82.5 61.9 %all-gather.5.cloned.1.call-done = bf16[512,8192]{1,0:T(8,128)(2,1)} async-done(((bf16[512,2048]{1,0:T(8,128)(2,1)}), bf16[512,8192]{1,0:T(8,128)(2,1)}) %all-gather.5.cloned.1.call-update) | async-done | bytes 8388624 | tf_op jit(solution)/shard_map/all_gather | solution.py:102
  146.4 3.9 while.271
  152.3 1.7 convolution_bitcast_fusion.50
  155.3 1.3 convolution_convert_fusion.5
  157.9 5.1 %while.269 = (s32[]{:T(128)}, f32[128,4]{0,1:T(4,128)}, f32[128,4]{0,1:T(4,128)}, f32[128,4,128]{2,0,1:T(8,128)S(1)}, s32[]{:T(128)}, /*index=5*/s32[]{:T(128)},...) while((s32[]{:T(128)}, f32[128,4]{0,1:T(4,128)}, ...), condition=%wide.region_68.69_spmd, body=%wide.region_65.68_spmd.sunk | while | flops 85329408 | bytes 3933329 | solution.py:73
  163.9 2.2 fusion.676
  166.0 1.6 fusion.691
  168.8 1.7 convolution_bitcast_fusion.49
  171.9 1.3 convolution_convert_fusion.3
  173.3 1.8 while.270
  176.0 2.2 fusion.685
  179.4 1.7 convolution_bitcast_fusion.51
  182.4 1.3 convolution_convert_fusion.7
  183.8 1.8 while.268
  186.5 2.2 fusion.690
  192.1 1.3 convolution_convert_fusion.9
  193.5 1.9 while.267
  196.3 1.3 fusion.689
  202.4 2.0 while.266
  204.6 2.2 fusion.688
  211.6 1.9 while.265
  220.5 1.8 while.264
  222.5 2.2 fusion.686
  229.5 1.9 while.263
  232.2 1.3 fusion.684
  238.4 1.8 while.262
  240.4 2.2 fusion.683
  244.0 1.3 convolution_convert_fusion.20
  246.7 1.8 while.261
  252.2 1.3 convolution_convert_fusion.22
  254.9 1.8 while.260
  260.3 1.3 convolution_convert_fusion.24
  263.1 1.8 while.259
  268.5 1.3 convolution_convert_fusion.26
  271.3 2.0 while.258
  276.9 1.3 convolution_convert_fusion.28
  278.3 1.3 convolution_convert_fusion.29
  279.7 1.8 while.257
  288.5 1.8 while.256
  303.2 12.5 %pmax.7 = bf16[128,64]{0,1:T(8,128)(2,1)S(1)} all-reduce(bf16[128,64]{0,1:T(8,128)(2,1)S(1)} %convert_element_type.488), channel_id=1, replica_groups=mesh['req'=64,'ctx'=4] {'ctx'}, use_global_device_ids=true, to_apply=%region_80.81 | all-reduce | flops 8192 | bytes 32768 | tf_op jit(solution)/shard_map/pmax | solution.py:143
  327.0 1.3 multiply_add_fusion.25
  363.8 3.0 copy.301
  367.6 44.2 %reduce-scatter.3.cloned.1.call-done = bf16[128,2048]{1,0:T(8,128)(2,1)} async-done(((bf16[128,8192]{1,0:T(8,128)(2,1)}), bf16[128,2048]{1,0:T(8,128)(2,1)}) %reduce-scatter.3.cloned.1.call-update) | async-done | bytes 524304 | tf_op jit(solution)/shard_map/reduce_scatter | solution.py:146
  412.2 2.2 fusion.337
  (559 shorter events, 192.5 us)
Async XLA Ops:
  6.5 74.6 %copy-start = (bf16[1,256,512]{2,1,0:T(8,128)(2,1)S(1)}, bf16[1,256,512]{2,1,0:T(8,128)(2,1)}, u32[]{:S(2)}) copy-start(bf16[1,256,512]{2,1,0:T(8,128)(2,1)} %param.43) | copy-start | bytes 786436
  6.5 71.7 %all-gather.3.cloned.1.call-start = ((), (), s32[]{:S(2)}) async-start(), calls=%async_computation.2 | async-start | bytes 10485760 | tf_op jit(solution)/shard_map/all_gather | solution.py:101
  7.3 137.1 %all-gather.5.cloned.1.call-start = ((), (), s32[]{:S(2)}) async-start(), calls=%async_computation.3 | async-start | bytes 10485760 | tf_op jit(solution)/shard_map/all_gather | solution.py:102
  8.0 358.8 %reduce-scatter.5.cloned.1.call-start = ((), (), s32[]{:S(2)}) async-start(), calls=%async_computation.5 | async-start | bytes 20480 | tf_op jit(solution)/shard_map/reduce_scatter | solution.py:152
  8.7 69.5 %copy-start.2 = (bf16[1,32,512]{2,1,0:T(8,128)(2,1)S(1)}, bf16[1,32,512]{2,1,0:T(8,128)(2,1)}, u32[]{:S(2)}) copy-start(bf16[1,32,512]{2,1,0:T(8,128)(2,1)} %param.45) | copy-start | bytes 98308
  17.3 129.1 %copy-start.1 = (bf16[1,256,64]{1,2,0:T(8,128)(2,1)S(1)}, bf16[1,256,64]{1,2,0:T(8,128)(2,1)}, u32[]{:S(2)}) copy-start(bf16[1,256,64]{1,2,0:T(8,128)(2,1)} %param.44) | copy-start | bytes 98308
  22.9 11.4 %copy-start.16 = (bf16[128,512]{0,1:T(8,128)(2,1)}, bf16[128,512]{0,1:T(8,128)(2,1)S(1)}, u32[]{:S(2)}) copy-start(bf16[128,512]{0,1:T(8,128)(2,1)S(1)} %get-tuple-element.3013) | copy-start | bytes 393220
  22.9 122.8 %copy-start.14 = (bf16[128,512]{0,1:T(8,128)(2,1)}, bf16[128,512]{0,1:T(8,128)(2,1)S(1)}, u32[]{:S(2)}) copy-start(bf16[128,512]{0,1:T(8,128)(2,1)S(1)} %get-tuple-element.3014) | copy-start | bytes 393220
  157.9 15.4 %copy-start.11 = (bf16[128,256]{0,1:T(8,128)(2,1)S(1)}, bf16[128,256]{0,1:T(8,128)(2,1)}, u32[]{:S(2)}) copy-start(bf16[128,256]{0,1:T(8,128)(2,1)} %copy.289) | copy-start | bytes 196612
  288.5 27.2 %copy-start.41 = (f32[128,4,32]{0,2,1:T(8,128)S(1)}, f32[128,4,32]{0,2,1:T(8,128)}, u32[]{:S(2)}) copy-start(f32[128,4,32]{0,2,1:T(8,128)} %get-tuple-element.3050) | copy-start | bytes 196612
  288.5 27.2 %copy-start.42 = (f32[128,4,32]{0,2,1:T(8,128)S(1)}, f32[128,4,32]{0,2,1:T(8,128)}, u32[]{:S(2)}) copy-start(f32[128,4,32]{0,2,1:T(8,128)} %get-tuple-element.3060) | copy-start | bytes 196612
  288.5 27.2 %copy-start.43 = (f32[128,4,32]{0,2,1:T(8,128)S(1)}, f32[128,4,32]{0,2,1:T(8,128)}, u32[]{:S(2)}) copy-start(f32[128,4,32]{0,2,1:T(8,128)} %get-tuple-element.3058) | copy-start | bytes 196612
  288.5 32.1 %copy-start.40 = (f32[128,4,32]{0,2,1:T(8,128)S(1)}, f32[128,4,32]{0,2,1:T(8,128)}, u32[]{:S(2)}) copy-start(f32[128,4,32]{0,2,1:T(8,128)} %get-tuple-element.3032) | copy-start | bytes 196612
  290.4 51.8 %copy-start.39 = (f32[128,4,128]{0,2,1:T(8,128)S(1)}, f32[128,4,128]{0,2,1:T(8,128)}, u32[]{:S(2)}) copy-start(f32[128,4,128]{0,2,1:T(8,128)} %copy.239) | copy-start | bytes 786436
  290.4 56.4 %copy-start.38 = (f32[128,4,128]{0,2,1:T(8,128)S(1)}, f32[128,4,128]{0,2,1:T(8,128)}, u32[]{:S(2)}) copy-start(f32[128,4,128]{0,2,1:T(8,128)} %copy.251) | copy-start | bytes 786436
  290.4 61.1 %copy-start.37 = (f32[128,4,128]{0,2,1:T(8,128)S(1)}, f32[128,4,128]{0,2,1:T(8,128)}, u32[]{:S(2)}) copy-start(f32[128,4,128]{0,2,1:T(8,128)} %copy.263) | copy-start | bytes 786436
  290.4 65.8 %copy-start.36 = (f32[128,4,128]{0,2,1:T(8,128)S(1)}, f32[128,4,128]{0,2,1:T(8,128)}, u32[]{:S(2)}) copy-start(f32[128,4,128]{0,2,1:T(8,128)} %copy.275) | copy-start | bytes 786436
  293.4 34.9 %copy-start.76 = (f32[128,4]{0,1:T(4,128)}, f32[128,4]{0,1:T(4,128)S(1)}, u32[]{:S(2)}) copy-start(f32[128,4]{0,1:T(4,128)S(1)} %max.143) | copy-start | bytes 6148
  294.8 33.6 %copy-start.78 = (f32[128,4]{0,1:T(4,128)}, f32[128,4]{0,1:T(4,128)S(1)}, u32[]{:S(2)}) copy-start(f32[128,4]{0,1:T(4,128)S(1)} %max.142) | copy-start | bytes 6148
  295.5 32.9 %copy-start.80 = (f32[128,4]{0,1:T(4,128)}, f32[128,4]{0,1:T(4,128)S(1)}, u32[]{:S(2)}) copy-start(f32[128,4]{0,1:T(4,128)S(1)} %max.141) | copy-start | bytes 6148
  296.1 32.2 %copy-start.82 = (f32[128,4]{0,1:T(4,128)}, f32[128,4]{0,1:T(4,128)S(1)}, u32[]{:S(2)}) copy-start(f32[128,4]{0,1:T(4,128)S(1)} %max.140) | copy-start | bytes 6148
  296.8 35.3 %copy-start.84 = (f32[128,4]{0,1:T(4,128)}, f32[128,4]{0,1:T(4,128)S(1)}, u32[]{:S(2)}) copy-start(f32[128,4]{0,1:T(4,128)S(1)} %max.139) | copy-start | bytes 6148
  297.5 34.6 %copy-start.86 = (f32[128,4]{0,1:T(4,128)}, f32[128,4]{0,1:T(4,128)S(1)}, u32[]{:S(2)}) copy-start(f32[128,4]{0,1:T(4,128)S(1)} %max.138) | copy-start | bytes 6148
  298.2 33.9 %copy-start.87 = (f32[128,4]{0,1:T(4,128)}, f32[128,4]{0,1:T(4,128)S(1)}, u32[]{:S(2)}) copy-start(f32[128,4]{0,1:T(4,128)S(1)} %max.137) | copy-start | bytes 6148
  298.9 33.2 %copy-start.88 = (f32[128,4]{0,1:T(4,128)}, f32[128,4]{0,1:T(4,128)S(1)}, u32[]{:S(2)}) copy-start(f32[128,4]{0,1:T(4,128)S(1)} %max.136) | copy-start | bytes 6148
  299.6 32.5 %copy-start.89 = (f32[128,4]{0,1:T(4,128)}, f32[128,4]{0,1:T(4,128)S(1)}, u32[]{:S(2)}) copy-start(f32[128,4]{0,1:T(4,128)S(1)} %max.135) | copy-start | bytes 6148
  300.3 31.9 %copy-start.90 = (f32[128,4]{0,1:T(4,128)}, f32[128,4]{0,1:T(4,128)S(1)}, u32[]{:S(2)}) copy-start(f32[128,4]{0,1:T(4,128)S(1)} %max.134) | copy-start | bytes 6148
  300.9 31.2 %copy-start.91 = (f32[128,4]{0,1:T(4,128)}, f32[128,4]{0,1:T(4,128)S(1)}, u32[]{:S(2)}) copy-start(f32[128,4]{0,1:T(4,128)S(1)} %max.133) | copy-start | bytes 6148
  301.7 30.5 %copy-start.92 = (f32[128,4]{0,1:T(4,128)}, f32[128,4]{0,1:T(4,128)S(1)}, u32[]{:S(2)}) copy-start(f32[128,4]{0,1:T(4,128)S(1)} %max.132) | copy-start | bytes 6148
  315.6 42.1 %copy-start.35 = (f32[128,4,128]{0,2,1:T(8,128)S(1)}, f32[128,4,128]{0,2,1:T(8,128)}, u32[]{:S(2)}) copy-start(f32[128,4,128]{0,2,1:T(8,128)} %copy.281) | copy-start | bytes 786436
  327.0 32.3 %copy-start.33 = (f32[128,4,128]{0,2,1:T(8,128)S(1)}, f32[128,4,128]{0,2,1:T(8,128)}, u32[]{:S(2)}) copy-start(f32[128,4,128]{0,2,1:T(8,128)} %copy.287) | copy-start | bytes 786436
  328.3 30.9 %copy-start.77 = (f32[128,4]{0,1:T(4,128)S(1)}, f32[128,4]{0,1:T(4,128)}, u32[]{:S(2)}) copy-start(f32[128,4]{0,1:T(4,128)} %copy-done.76) | copy-start | bytes 6148
  329.2 82.7 %reduce-scatter.3.cloned.1.call-start = ((), (), s32[]{:S(2)}) async-start(), calls=%async_computation.4 | async-start | bytes 2621440 | tf_op jit(solution)/shard_map/reduce_scatter | solution.py:146
  329.2 17.6 %copy-start.100 = (f32[128,4]{0,1:T(4,128)S(1)}, f32[128,4]{0,1:T(4,128)}, u32[]{:S(2)}) copy-start(f32[128,4]{0,1:T(4,128)} %get-tuple-element.3064) | copy-start | bytes 6148
  329.2 20.0 %copy-start.99 = (f32[128,4]{0,1:T(4,128)S(1)}, f32[128,4]{0,1:T(4,128)}, u32[]{:S(2)}) copy-start(f32[128,4]{0,1:T(4,128)} %get-tuple-element.2950) | copy-start | bytes 6148
  329.2 22.3 %copy-start.97 = (f32[128,4]{0,1:T(4,128)S(1)}, f32[128,4]{0,1:T(4,128)}, u32[]{:S(2)}) copy-start(f32[128,4]{0,1:T(4,128)} %get-tuple-element.3076) | copy-start | bytes 6148
  329.2 24.6 %copy-start.83 = (f32[128,4]{0,1:T(4,128)S(1)}, f32[128,4]{0,1:T(4,128)}, u32[]{:S(2)}) copy-start(f32[128,4]{0,1:T(4,128)} %copy-done.82) | copy-start | bytes 6148
  329.2 24.6 %copy-start.95 = (f32[128,4]{0,1:T(4,128)S(1)}, f32[128,4]{0,1:T(4,128)}, u32[]{:S(2)}) copy-start(f32[128,4]{0,1:T(4,128)} %get-tuple-element.2946) | copy-start | bytes 6148
  329.3 27.0 %copy-start.81 = (f32[128,4]{0,1:T(4,128)S(1)}, f32[128,4]{0,1:T(4,128)}, u32[]{:S(2)}) copy-start(f32[128,4]{0,1:T(4,128)} %copy-done.80) | copy-start | bytes 6148
  329.3 27.0 %copy-start.96 = (f32[128,4]{0,1:T(4,128)S(1)}, f32[128,4]{0,1:T(4,128)}, u32[]{:S(2)}) copy-start(f32[128,4]{0,1:T(4,128)} %get-tuple-element.3074) | copy-start | bytes 6148
  329.3 28.4 %copy-start.79 = (f32[128,4]{0,1:T(4,128)S(1)}, f32[128,4]{0,1:T(4,128)}, u32[]{:S(2)}) copy-start(f32[128,4]{0,1:T(4,128)} %copy-done.78) | copy-start | bytes 6148
  329.3 28.4 %copy-start.94 = (f32[128,4]{0,1:T(4,128)S(1)}, f32[128,4]{0,1:T(4,128)}, u32[]{:S(2)}) copy-start(f32[128,4]{0,1:T(4,128)} %get-tuple-element.2942) | copy-start | bytes 6148
  330.8 30.6 %copy-start.34 = (f32[128,4,128]{0,2,1:T(8,128)S(1)}, f32[128,4,128]{0,2,1:T(8,128)}, u32[]{:S(2)}) copy-start(f32[128,4,128]{0,2,1:T(8,128)} %copy.293) | copy-start | bytes 786436
  330.8 30.6 %copy-start.93 = (f32[128,4]{0,1:T(4,128)S(1)}, f32[128,4]{0,1:T(4,128)}, u32[]{:S(2)}) copy-start(f32[128,4]{0,1:T(4,128)} %get-tuple-element.2938) | copy-start | bytes 6148
  333.4 18.1 %copy-start.85 = (f32[128,4]{0,1:T(4,128)S(1)}, f32[128,4]{0,1:T(4,128)}, u32[]{:S(2)}) copy-start(f32[128,4]{0,1:T(4,128)} %copy-done.84) | copy-start | bytes 6148
  333.4 29.5 %copy-start.32 = (f32[128,4,128]{0,2,1:T(8,128)S(1)}, f32[128,4,128]{0,2,1:T(8,128)}, u32[]{:S(2)}) copy-start(f32[128,4,128]{0,2,1:T(8,128)} %copy.299) | copy-start | bytes 786436
  333.4 29.5 %copy-start.98 = (f32[128,4]{0,1:T(4,128)S(1)}, f32[128,4]{0,1:T(4,128)}, u32[]{:S(2)}) copy-start(f32[128,4]{0,1:T(4,128)} %get-tuple-element.2936) | copy-start | bytes 6148
  334.7 28.5 %copy-start.61 = (f32[128,64]{0,1:T(8,128)S(1)}, f32[128,64]{0,1:T(8,128)}, u32[]{:S(2)}) copy-start(f32[128,64]{0,1:T(8,128)} %get-tuple-element.2934) | copy-start | bytes 98308
  (57 other events, 303.5 us)
Sparse Core Ops, SparseCore 0:
  9.1 69.0 all-gather.2
  80.0 64.3 all-gather.4
  329.3 32.8 reduce-scatter.4
  367.0 44.8 reduce-scatter.2
where the time goes:
time: 426 us; the launch traced here: 421 us
  waiting for transfers between devices  151 us (35%)
  matrix products  151 us (35%)
  local copies, waits for them, and re-layouts  44.5 us (10%)
  other arithmetic  43.7 us (10%)
  between operations  16.3 us (4%)
  blocking collectives  12.5 us (3%)
    all_gather x1, waiting for transfers between devices, shards(): lax.all_gather(w_value, 'ctx', axis=1, tiled=True)  61.9 us
    reduce_scatter x1, waiting for transfers between devices, shards(): lax.psum_scatter((running_out * factor[..., None]).reshape(query_count, H...  44.2 us
    all_gather x1, waiting for transfers between devices, shards(): lax.all_gather(w_key, 'ctx', axis=1, tiled=True)  43.7 us
    dot_general x32, matrix products, expand_block(): jnp.dot(lat_rows, weight_value, preferred_element_type=jnp.float32)  41.1 us
    dot_general x32, matrix products, expand_block(): jnp.dot(lat_rows, weight_key, preferred_element_type=jnp.float32)  41 us
    dot_general x32, matrix products, expand_block(): jnp.einsum('qhd,kd->qhk', query_rope, rope_keys, preferred_element_type=j...  32.5 us
    while x32, local copies, waits for them, and re-layouts, cached_pass(): return lax.fori_loop(0, block_count, advance, running)  22 us
    dot_general x32, matrix products, expand_block(): jnp.einsum('qhk,khd->qhd', weights.astype(jnp.bfloat16), value_rows, pref...  20.2 us
  transfers between devices with their start and end apart: 4, of which 3 were waited for; matrix products, arithmetic and copies ran while one was open for 16% of the time, Pallas kernels for 0%

commit v1 on v0

--- a/solution.py
+++ b/solution.py
@@ -11,6 +11,13 @@
 GROUP = 4
 BLOCK = 256
 blocked_score = -1e30
+
+
+def exchange_gather(array, axis, dim):
+    size = lax.axis_size(axis)
+    parts = jnp.stack([array for _ in range(size)])
+    parts = lax.all_to_all(parts, axis, split_axis=0, concat_axis=0)
+    return jnp.concatenate(parts, axis=dim)
 
 
 def expand_block(
@@ -99,7 +106,7 @@
     live_rows = lengths[0, 0]
     full_key, full_value = (
         lax.all_gather(w_key, "ctx", axis=1, tiled=True),
-        lax.all_gather(w_value, "ctx", axis=1, tiled=True),
+        exchange_gather(w_value, "ctx", 1),
     )
     maxima = []
     sums = []

time: 426 us -> 572 us (1.34)
  matrix products: 151 us -> 228 us
  local copies, waits for them, and re-layouts: 44.5 us -> 80.3 us
  other arithmetic: 43.7 us -> 60.4 us
  starting transfers between devices: 0.12 us -> 8.9 us
  waiting for transfers between devices: 151 us -> 159 us
    all_to_all x0 -> x1, waiting for transfers between devices: none -> 101 us  [exchange_gather(): parts = lax.all_to_all(parts, axis, split_axis=0, concat_axis=0)]
    all_gather x1 -> x0, waiting for transfers between devices: 61.9 us -> none  [shards(): lax.all_gather(w_value, 'ctx', axis=1, tiled=True)]
    all_gather x1, waiting for transfers between devices: 43.7 us -> 0.01 us  [shards(): lax.all_gather(w_key, 'ctx', axis=1, tiled=True)]
    dot_general x32, matrix products: 16.5 us -> 37 us  [expand_block(): jnp.einsum('qhd,khd->qhk', query_nope, key_rows, preferred_element_type=j...]
    dot_general x32, matrix products: 32.5 us -> 51.2 us  [expand_block(): jnp.einsum('qhd,kd->qhk', query_rope, rope_keys, preferred_element_type=j...]
    another operation x49 -> x50, local copies, waits for them, and re-layouts: 2.12 us -> 20 us
    dot_general x32, matrix products: 41.1 us -> 56 us  [expand_block(): jnp.dot(lat_rows, weight_value, preferred_element_type=jnp.float32)]
    dot_general x32, matrix products: 41 us -> 52.5 us  [expand_block(): jnp.dot(lat_rows, weight_key, preferred_element_type=jnp.float32)]
  transfers between devices with their start and end apart: 4 -> 4, of which waited for: 3 -> 3; matrix products, arithmetic and copies ran while one was open for 16% -> 22% of each run, Pallas kernels for 0% -> 0%
where the time goes in v1:
time: 572 us; the launch traced here: 564 us
  matrix products  228 us (40%)
  waiting for transfers between devices  159 us (28%)
  local copies, waits for them, and re-layouts  80.3 us (14%)
  other arithmetic  60.4 us (11%)
  between operations  14.6 us (3%)
  blocking collectives  12.5 us (2%)
  starting transfers between devices  8.9 us (2%)
    all_to_all x1, waiting for transfers between devices, exchange_gather(): parts = lax.all_to_all(parts, axis, split_axis=0, concat_axis=0)  101 us
    dot_general x32, matrix products, expand_block(): jnp.dot(lat_rows, weight_value, preferred_element_type=jnp.float32)  56 us
    dot_general x32, matrix products, expand_block(): jnp.dot(lat_rows, weight_key, preferred_element_type=jnp.float32)  52.5 us
    dot_general x32, matrix products, expand_block(): jnp.einsum('qhd,kd->qhk', query_rope, rope_keys, preferred_element_type=j...  51.2 us
    reduce_scatter x1, waiting for transfers between devices, shards(): lax.psum_scatter((running_out * factor[..., None]).reshape(query_count, H...  45.1 us
    dot_general x32, matrix products, expand_block(): jnp.einsum('qhd,khd->qhk', query_nope, key_rows, preferred_element_type=j...  37 us
    dot_general x32, matrix products, expand_block(): jnp.einsum('qhk,khd->qhd', weights.astype(jnp.bfloat16), value_rows, pref...  31.2 us
    while x32, local copies, waits for them, and re-layouts, cached_pass(): return lax.fori_loop(0, block_count, advance, running)  30.4 us
  transfers between devices with their start and end apart: 4, of which 3 were waited for; matrix products, arithmetic and copies ran while one was open for 22% of the time, Pallas kernels for 0%

profile of v1, /device:TPU:1, one launch (start us, length us, event | category | flops | bytes accessed | tf_op | source)
XLA Modules:
  0.0 563.8 jit_solution(12869595617031397651)
XLA Ops:
  7.3 2.9 copy.206
  10.1 3.9 stack.2
  14.0 8.8 %all-to-all-start = ((bf16[4,512,2048]{1,2,0:T(8,128)(2,1)}), bf16[4,512,2048]{1,2,0:T(8,128)(2,1)}, u32[]{:S(2)}, u32[]{:S(2)}) async-start(bf16[4,512,2048]{1,2,0:T(8,128)(2,1)} %stack.2), calls=%async_computation | async-start | bytes 16777216 | tf_op jit(solution)/shard_map/all_to_all | solution.py:19
  23.6 3.4 copy.204
  60.0 101.5 %all-to-all-done = bf16[4,512,2048]{1,2,0:T(8,128)(2,1)} async-done(((bf16[4,512,2048]{1,2,0:T(8,128)(2,1)}), bf16[4,512,2048]{1,2,0:T(8,128)(2,1)}, u32[]{:S(2)}, u32[]{:S(2)}) %all-to-all-start) | async-done | bytes 8388640 | tf_op jit(solution)/shard_map/all_to_all | solution.py:19
  207.4 2.1 convolution_convert_fusion.4
  209.5 2.1 convolution_convert_fusion.10
  211.5 2.1 convolution_convert_fusion.12
  213.6 2.1 convolution_convert_fusion.14
  215.7 2.1 convolution_convert_fusion.2
  219.9 3.6 while.256
  229.1 4.9 while.257
  236.3 2.2 fusion.677
  238.5 2.2 fusion.678
  243.9 6.1 %while.258 = (s32[]{:T(128)}, f32[128,4]{0,1:T(4,128)}, f32[128,4]{0,1:T(4,128)}, f32[128,4,128]{2,0,1:T(8,128)S(1)}, s32[]{:T(128)}, /*index=5*/s32[]{:T(128)},...) while((s32[]{:T(128)}, f32[128,4]{0,1:T(4,128)}, ...), condition=%wide.region_13.14_spmd, body=%wide.region_10.13_spmd.sunk | while | flops 85329408 | bytes 3933329 | solution.py:80
  252.3 2.1 fusion.679
  257.1 4.8 while.259
  264.2 2.2 fusion.680
  269.7 6.1 %while.260 = (s32[]{:T(128)}, f32[128,4]{0,1:T(4,128)}, f32[128,4]{0,1:T(4,128)}, f32[128,4,128]{2,0,1:T(8,128)S(1)}, s32[]{:T(128)}, /*index=5*/s32[]{:T(128)},...) while((s32[]{:T(128)}, f32[128,4]{0,1:T(4,128)}, ...), condition=%wide.region_23.24_spmd, body=%wide.region_20.23_spmd.sunk | while | flops 85329408 | bytes 3933329 | solution.py:80
  278.1 2.2 fusion.681
  282.8 4.7 while.261
  289.9 2.2 fusion.682
  295.2 5.9 %while.262 = (s32[]{:T(128)}, f32[128,4]{0,1:T(4,128)}, f32[128,4]{0,1:T(4,128)}, f32[128,4,128]{2,0,1:T(8,128)S(1)}, s32[]{:T(128)}, /*index=5*/s32[]{:T(128)},...) while((s32[]{:T(128)}, f32[128,4]{0,1:T(4,128)}, ...), condition=%wide.region_33.34_spmd, body=%wide.region_30.33_spmd.sunk | while | flops 85329408 | bytes 3933329 | solution.py:80
  303.4 2.2 fusion.683
  308.2 4.8 while.263
  315.4 2.2 fusion.684
  320.2 4.9 while.271
  327.4 2.2 fusion.676
  332.8 6.1 %while.267 = (s32[]{:T(128)}, f32[128,4]{0,1:T(4,128)}, f32[128,4]{0,1:T(4,128)}, f32[128,4,128]{2,0,1:T(8,128)S(1)}, s32[]{:T(128)}, /*index=5*/s32[]{:T(128)},...) while((s32[]{:T(128)}, f32[128,4]{0,1:T(4,128)}, ...), condition=%wide.region_58.59_spmd, body=%wide.region_55.58_spmd.sunk | while | flops 85329408 | bytes 3933329 | solution.py:80
  341.2 2.2 fusion.689
  346.6 6.0 %while.268 = (s32[]{:T(128)}, f32[128,4]{0,1:T(4,128)}, f32[128,4]{0,1:T(4,128)}, f32[128,4,128]{2,0,1:T(8,128)S(1)}, s32[]{:T(128)}, /*index=5*/s32[]{:T(128)},...) while((s32[]{:T(128)}, f32[128,4]{0,1:T(4,128)}, ...), condition=%wide.region_63.64_spmd, body=%wide.region_60.63_spmd.sunk | while | flops 85329408 | bytes 3933329 | solution.py:80
  354.9 2.1 fusion.690
  360.2 7.0 %while.269 = (s32[]{:T(128)}, f32[128,4]{0,1:T(4,128)}, f32[128,4]{0,1:T(4,128)}, f32[128,4,128]{2,0,1:T(8,128)S(1)}, s32[]{:T(128)}, /*index=5*/s32[]{:T(128)},...) while((s32[]{:T(128)}, f32[128,4]{0,1:T(4,128)}, ...), condition=%wide.region_68.69_spmd, body=%wide.region_65.68_spmd.sunk | while | flops 85329408 | bytes 3933329 | solution.py:80
  369.6 2.2 fusion.691
  375.7 7.8 %while.266 = (s32[]{:T(128)}, f32[128,4]{0,1:T(4,128)}, f32[128,4]{0,1:T(4,128)}, f32[128,4,128]{2,0,1:T(8,128)}, s32[]{:T(128)}, /*index=5*/s32[]{:T(128)}, bf1...) while((s32[]{:T(128)}, f32[128,4]{0,1:T(4,128)}, ...), condition=%wide.region_53.54_spmd, body=%wide.region_50.53_spmd.sunk | while | flops 85329408 | bytes 3933329 | solution.py:80
  380.8 2.1 fusion.1057
  385.8 2.2 fusion.688
  391.2 7.0 %while.265 = (s32[]{:T(128)}, f32[128,4]{0,1:T(4,128)}, f32[128,4]{0,1:T(4,128)}, f32[128,4,128]{2,0,1:T(8,128)S(1)}, s32[]{:T(128)}, /*index=5*/s32[]{:T(128)},...) while((s32[]{:T(128)}, f32[128,4]{0,1:T(4,128)}, ...), condition=%wide.region_48.49_spmd, body=%wide.region_45.48_spmd.sunk | while | flops 85329408 | bytes 3933329 | solution.py:80
  400.6 2.2 fusion.687
  406.7 7.7 %while.264 = (s32[]{:T(128)}, f32[128,4]{0,1:T(4,128)}, f32[128,4]{0,1:T(4,128)}, f32[128,4,128]{2,0,1:T(8,128)}, s32[]{:T(128)}, /*index=5*/s32[]{:T(128)}, bf1...) while((s32[]{:T(128)}, f32[128,4]{0,1:T(4,128)}, ...), condition=%wide.region_43.44_spmd, body=%wide.region_40.43_spmd.sunk | while | flops 85329408 | bytes 3933329 | solution.py:80
  411.7 2.1 fusion.1037
  416.7 2.2 fusion.686
  422.1 6.2 %while.270 = (s32[]{:T(128)}, f32[128,4]{0,1:T(4,128)}, f32[128,4]{0,1:T(4,128)}, f32[128,4,128]{2,0,1:T(8,128)S(1)}, s32[]{:T(128)}, /*index=5*/s32[]{:T(128)},...) while((s32[]{:T(128)}, f32[128,4]{0,1:T(4,128)}, ...), condition=%wide.region_73.74_spmd, body=%wide.region_70.73_spmd.sunk | while | flops 85329408 | bytes 3933329 | solution.py:80
  454.0 12.5 %pmax.7 = bf16[128,64]{0,1:T(8,128)(2,1)S(1)} all-reduce(bf16[128,64]{0,1:T(8,128)(2,1)S(1)} %convert_element_type.488), channel_id=1, replica_groups=mesh['req'=64,'ctx'=4] {'ctx'}, use_global_device_ids=true, to_apply=%region_80.81 | all-reduce | flops 8192 | bytes 32768 | tf_op jit(solution)/shard_map/pmax | solution.py:150
  494.5 3.0 copy.302
  497.5 11.4 %reduce-scatter.5.cloned.1.call-done = bf16[128,16]{0,1:T(8,128)(2,1)} async-done(((bf16[128,64]{0,1:T(8,128)(2,1)}), bf16[128,16]{0,1:T(8,128)(2,1)}) %reduce-scatter.5.cloned.1.call-update) | async-done | bytes 4112 | tf_op jit(solution)/shard_map/reduce_scatter | solution.py:159
  509.7 45.1 %reduce-scatter.3.cloned.1.call-done = bf16[128,2048]{1,0:T(8,128)(2,1)} async-done(((bf16[128,8192]{1,0:T(8,128)(2,1)}), bf16[128,2048]{1,0:T(8,128)(2,1)}) %reduce-scatter.3.cloned.1.call-update) | async-done | bytes 524304 | tf_op jit(solution)/shard_map/reduce_scatter | solution.py:153
  555.1 2.2 fusion.337
  (408 shorter events, 306.8 us)
Async XLA Ops:
  6.5 185.6 %copy-start = (bf16[1,256,512]{2,1,0:T(8,128)(2,1)S(1)}, bf16[1,256,512]{2,1,0:T(8,128)(2,1)}, u32[]{:S(2)}) copy-start(bf16[1,256,512]{2,1,0:T(8,128)(2,1)} %param.43) | copy-start | bytes 786436
  6.5 211.2 %all-gather.2.cloned.1.call-start = ((), (), s32[]{:S(2)}) async-start(), calls=%async_computation.3 | async-start | bytes 10485760 | tf_op jit(solution)/shard_map/all_gather | solution.py:108
  14.0 147.5 %all-to-all-start = ((bf16[4,512,2048]{1,2,0:T(8,128)(2,1)}), bf16[4,512,2048]{1,2,0:T(8,128)(2,1)}, u32[]{:S(2)}, u32[]{:S(2)}) async-start(bf16[4,512,2048]{1,2,0:T(8,128)(2,1)} %stack.2), calls=%async_computation | async-start | bytes 16777216 | tf_op jit(solution)/shard_map/all_to_all | solution.py:19
  22.9 486.0 %reduce-scatter.5.cloned.1.call-start = ((), (), s32[]{:S(2)}) async-start(), calls=%async_computation.5 | async-start | bytes 20480 | tf_op jit(solution)/shard_map/reduce_scatter | solution.py:159
  23.5 138.0 %copy-start.2 = (bf16[1,32,512]{2,1,0:T(8,128)(2,1)S(1)}, bf16[1,32,512]{2,1,0:T(8,128)(2,1)}, u32[]{:S(2)}) copy-start(bf16[1,32,512]{2,1,0:T(8,128)(2,1)} %param.45) | copy-start | bytes 98308
  28.0 162.2 %copy-start.6 = (bf16[128,512]{0,1:T(8,128)(2,1)}, bf16[128,512]{0,1:T(8,128)(2,1)S(1)}, u32[]{:S(2)}) copy-start(bf16[128,512]{0,1:T(8,128)(2,1)S(1)} %get-tuple-element.3001) | copy-start | bytes 393220
  28.0 162.2 %copy-start.7 = (bf16[128,512]{0,1:T(8,128)(2,1)}, bf16[128,512]{0,1:T(8,128)(2,1)S(1)}, u32[]{:S(2)}) copy-start(bf16[128,512]{0,1:T(8,128)(2,1)S(1)} %get-tuple-element.3006) | copy-start | bytes 393220
  28.0 162.2 %copy-start.8 = (bf16[128,512]{0,1:T(8,128)(2,1)}, bf16[128,512]{0,1:T(8,128)(2,1)S(1)}, u32[]{:S(2)}) copy-start(bf16[128,512]{0,1:T(8,128)(2,1)S(1)} %get-tuple-element.3005) | copy-start | bytes 393220
  28.0 162.2 %copy-start.9 = (bf16[128,512]{0,1:T(8,128)(2,1)}, bf16[128,512]{0,1:T(8,128)(2,1)S(1)}, u32[]{:S(2)}) copy-start(bf16[128,512]{0,1:T(8,128)(2,1)S(1)} %get-tuple-element.3004) | copy-start | bytes 393220
  28.0 162.2 %copy-start.10 = (bf16[128,512]{0,1:T(8,128)(2,1)}, bf16[128,512]{0,1:T(8,128)(2,1)S(1)}, u32[]{:S(2)}) copy-start(bf16[128,512]{0,1:T(8,128)(2,1)S(1)} %get-tuple-element.2999) | copy-start | bytes 393220
  28.0 162.2 %copy-start.11 = (bf16[128,512]{0,1:T(8,128)(2,1)}, bf16[128,512]{0,1:T(8,128)(2,1)S(1)}, u32[]{:S(2)}) copy-start(bf16[128,512]{0,1:T(8,128)(2,1)S(1)} %get-tuple-element.3002) | copy-start | bytes 393220
  28.0 162.2 %copy-start.12 = (bf16[128,512]{0,1:T(8,128)(2,1)}, bf16[128,512]{0,1:T(8,128)(2,1)S(1)}, u32[]{:S(2)}) copy-start(bf16[128,512]{0,1:T(8,128)(2,1)S(1)} %get-tuple-element.3003) | copy-start | bytes 393220
  28.0 162.2 %copy-start.13 = (bf16[128,512]{0,1:T(8,128)(2,1)}, bf16[128,512]{0,1:T(8,128)(2,1)S(1)}, u32[]{:S(2)}) copy-start(bf16[128,512]{0,1:T(8,128)(2,1)S(1)} %get-tuple-element.3000) | copy-start | bytes 393220
  194.9 24.9 %copy-start.1 = (bf16[1,256,64]{1,2,0:T(8,128)(2,1)S(1)}, bf16[1,256,64]{1,2,0:T(8,128)(2,1)}, u32[]{:S(2)}) copy-start(bf16[1,256,64]{1,2,0:T(8,128)(2,1)} %param.44) | copy-start | bytes 98308
  223.5 5.6 copy-start.18
  223.5 5.6 copy-start.24
  229.1 7.2 %copy-start.5 = (bf16[1,32,64]{2,1,0:T(8,128)(2,1)S(1)}, bf16[1,32,64]{2,1,0:T(8,128)(2,1)}, u32[]{:S(2)}) copy-start(bf16[1,32,64]{2,1,0:T(8,128)(2,1)} %param.46) | copy-start | bytes 12292
  234.0 9.9 %copy-start.19 = (f32[128,4]{0,1:T(4,128)}, f32[128,4]{0,1:T(4,128)S(1)}, u32[]{:S(2)}) copy-start(f32[128,4]{0,1:T(4,128)S(1)} %get-tuple-element.2312) | copy-start | bytes 6148
  261.9 7.7 %copy-start.20 = (f32[128,4]{0,1:T(4,128)}, f32[128,4]{0,1:T(4,128)S(1)}, u32[]{:S(2)}) copy-start(f32[128,4]{0,1:T(4,128)S(1)} %get-tuple-element.2316) | copy-start | bytes 6148
  287.6 7.6 %copy-start.21 = (f32[128,4]{0,1:T(4,128)}, f32[128,4]{0,1:T(4,128)S(1)}, u32[]{:S(2)}) copy-start(f32[128,4]{0,1:T(4,128)S(1)} %get-tuple-element.2320) | copy-start | bytes 6148
  313.1 6.5 %copy-start.22 = (f32[128,4]{0,1:T(4,128)}, f32[128,4]{0,1:T(4,128)S(1)}, u32[]{:S(2)}) copy-start(f32[128,4]{0,1:T(4,128)S(1)} %get-tuple-element.2324) | copy-start | bytes 6148
  367.2 8.5 %copy-start.3 = (f32[128,4,128]{2,0,1:T(8,128)}, f32[128,4,128]{2,0,1:T(8,128)S(1)}, u32[]{:S(2)}) copy-start(f32[128,4,128]{2,0,1:T(8,128)S(1)} %get-tuple-element.2335) | copy-start | bytes 786436
  398.2 8.5 %copy-start.4 = (f32[128,4,128]{2,0,1:T(8,128)}, f32[128,4,128]{2,0,1:T(8,128)S(1)}, u32[]{:S(2)}) copy-start(f32[128,4,128]{2,0,1:T(8,128)S(1)} %get-tuple-element.2327) | copy-start | bytes 786436
  432.0 21.2 %copy-start.17 = (f32[128,4]{0,1:T(4,128)S(1)}, f32[128,4]{0,1:T(4,128)}, u32[]{:S(2)}) copy-start(f32[128,4]{0,1:T(4,128)} %get-tuple-element.2338) | copy-start | bytes 6148
  432.0 35.7 %copy-start.15 = (f32[128,4,32]{0,2,1:T(8,128)S(1)}, f32[128,4,32]{0,2,1:T(8,128)}, u32[]{:S(2)}) copy-start(f32[128,4,32]{0,2,1:T(8,128)} %get-tuple-element.3036) | copy-start | bytes 196612
  432.0 41.8 %copy-start.23 = (f32[128,4]{0,1:T(4,128)S(1)}, f32[128,4]{0,1:T(4,128)}, u32[]{:S(2)}) copy-start(f32[128,4]{0,1:T(4,128)} %get-tuple-element.2355) | copy-start | bytes 6148
  438.0 42.3 %copy-start.16 = (f32[128,4,32]{0,2,1:T(8,128)S(1)}, f32[128,4,32]{0,2,1:T(8,128)}, u32[]{:S(2)}) copy-start(f32[128,4,32]{0,2,1:T(8,128)} %get-tuple-element.3042) | copy-start | bytes 196612
  438.0 44.8 %copy-start.14 = (f32[128,4,128]{0,2,1:T(8,128)S(1)}, f32[128,4,128]{0,2,1:T(8,128)}, u32[]{:S(2)}) copy-start(f32[128,4,128]{0,2,1:T(8,128)} %copy.246) | copy-start | bytes 786436
  475.3 79.5 %reduce-scatter.3.cloned.1.call-start = ((), (), s32[]{:S(2)}) async-start(), calls=%async_computation.4 | async-start | bytes 2621440 | tf_op jit(solution)/shard_map/reduce_scatter | solution.py:153
Sparse Core Ops, SparseCore 0:
  9.1 114.0 all-gather.1
  475.4 33.4 reduce-scatter.4
  511.7 43.0 reduce-scatter.2
